TPU v7x, 128 devices: a whole 4x4x4 slice. The times are simulated.
128 devices in a mesh: dp: 16 (over z, y), mp: 8 (over x, core).
Axes of the slice: x: 4, y: 4, z: 4, core: 2. Of those that a mesh axis runs over, the one named last changes fastest.
Arguments:
- cotangent: bfloat16 [32768, 4096], P('dp'), may hold values from -64 to 64, as said below
- activation: bfloat16 [32768, 8192], P('dp', 'mp'), may hold values from -64 to 64, as said below
Outputs:
- update: bfloat16 [4096, 8192], P('dp', 'mp')
Inputs may be any that keep to these rules, and one draw needn't show every extreme that they name: `cotangent`: real-valued entries. `activation`: real-valued entries.
All inputs are finite; a program needn't handle non-finite values.
Results may differ from a plain program's by a relative error of at most 0.0054.
Values may be sent and summed in bfloat16 or wider, within the bound.
A program may use at most 256 MiB of HBM per device.

v0:
```python
import math
import jax
import jax.numpy as jnp
from jax import lax
from jax.sharding import PartitionSpec as P

N = 8192
ROWS = 4096
LINEAR_COEF = 3.4445
CUBIC_COEF = -4.775
QUINTIC_COEF = 2.0315
NORM_EPSILON = 1e-07
NORM_SHARE = 0.25
CONTRACT_FIRST = (((0,), (0,)), ((), ()))
CONTRACT_LAST = (((1,), (1,)), ((), ()))


def local(cotangent, activation):
    section = cotangent
    gradient = lax.psum_scatter(
        lax.dot_general(section, activation, CONTRACT_FIRST, preferred_element_type=jnp.float32),
        "dp",
        scatter_dimension=0,
        tiled=True,
    )
    sum_squares = lax.psum(jnp.sum(gradient * gradient), ("dp", "mp"))
    factor = NORM_SHARE * math.sqrt(ROWS) / (jnp.sqrt(sum_squares) + NORM_EPSILON)
    normalized = (gradient * factor).astype(jnp.bfloat16)
    weight_column = lax.all_gather(normalized, "dp", axis=0, tiled=True)
    section = weight_column
    gram_tile = lax.psum_scatter(
        lax.dot_general(section, normalized, CONTRACT_LAST, preferred_element_type=jnp.float32),
        "mp",
        scatter_dimension=0,
        tiled=True,
    ).T.astype(jnp.bfloat16)
    row_panel = lax.all_gather(gram_tile, "mp", axis=1, tiled=True)
    section = row_panel
    square_tile = jnp.dot(
        section,
        lax.all_gather(gram_tile, "dp", axis=0, tiled=True),
        preferred_element_type=jnp.float32,
    )
    polynomial = (CUBIC_COEF * gram_tile.astype(jnp.float32) + QUINTIC_COEF * square_tile).astype(
        jnp.bfloat16
    )
    section = weight_column
    product_tile = jnp.dot(
        lax.all_gather(polynomial, "mp", axis=1, tiled=True),
        section,
        preferred_element_type=jnp.float32,
    )
    rescale = math.sqrt(N)
    return (rescale * (LINEAR_COEF * normalized.astype(jnp.float32) + product_tile)).astype(
        jnp.bfloat16
    )


def solution(mesh):
    return jax.shard_map(
        local,
        mesh=mesh,
        in_specs=(P("dp", None), P("dp", "mp")),
        out_specs=P("dp", "mp"),
        check_vma=False,
    )
```

profile of v0, /device:TPU:1, one launch (start us, length us, event | category | flops | bytes accessed | tf_op | source)
XLA Modules:
  0.0 457.3 jit_solution(6413023268243869418)
XLA Ops:
  6.5 0.0 reduce-scatter.3.cloned.1.call-start
  6.5 23.7 %fusion.4 = f32[4096,1024]{1,0:T(8,128)} fusion(bf16[2048,4096]{1,0:T(8,128)(2,1)} %param.2, bf16[2048,1024]{1,0:T(8,128)(2,1)} %param.3), kind=kOutput, calls=%fused_computation.9 | convolution fusion | flops 17179869184 | bytes 37748736 | tf_op jit(solution)/shard_map/dot_general | solution.py:21
  30.3 0.0 reduce-scatter.3.cloned.1.call-update
  30.3 0.0 all-gather.5.cloned.1.call-start
  30.3 113.7 %reduce-scatter.3.cloned.1.call-done = f32[256,1024]{1,0:T(8,128)} async-done(((f32[4096,1024]{1,0:T(8,128)}), f32[256,1024]{1,0:T(8,128)}) %reduce-scatter.3.cloned.1.call-update) | async-done | bytes 1048592 | tf_op jit(solution)/shard_map/reduce_scatter | solution.py:20
  144.0 2.1 multiply_reduce_fusion
  146.1 64.8 %psum.7 = f32[]{:T(128)} all-reduce(f32[]{:T(128)} %multiply_reduce_fusion), channel_id=1, replica_groups=mesh['dp'=16,'mp'=8] {'dp','mp'}, use_global_device_ids=true, to_apply=%region_2.0 | all-reduce | flops 1 | bytes 8 | tf_op jit(solution)/shard_map/psum | solution.py:26
  211.6 2.1 multiply_convert_fusion
  213.7 0.0 all-gather.5.cloned.1.call-update
  213.7 0.0 reduce-scatter.5.cloned.1.call-start
  213.8 68.2 %all-gather.5.cloned.1.call-done = bf16[4096,1024]{1,0:T(8,128)(2,1)} async-done(((bf16[256,1024]{1,0:T(8,128)(2,1)}), bf16[4096,1024]{1,0:T(8,128)(2,1)}) %all-gather.5.cloned.1.call-update) | async-done | bytes 8388624 | tf_op jit(solution)/shard_map/all_gather | solution.py:29
  282.0 7.8 %fusion.5 = f32[4096,256]{1,0:T(8,128)} fusion(bf16[4096,1024]{1,0:T(8,128)(2,1)} %all-gather.5.cloned.1.call-done, bf16[256,1024]{1,0:T(8,128)(2,1)} %multiply_convert_fusion), kind=kOutput, calls=%fused_computation.10 | convolution fusion | flops 2147483648 | bytes 13107200 | tf_op jit(solution)/shard_map/dot_general | solution.py:32
  289.8 0.0 reduce-scatter.5.cloned.1.call-update
  289.8 0.0 all-gather.7.cloned.1.call-start
  289.9 34.7 %reduce-scatter.5.cloned.1.call-done = f32[512,256]{1,0:T(8,128)} async-done(((f32[4096,256]{1,0:T(8,128)}), f32[512,256]{1,0:T(8,128)}) %reduce-scatter.5.cloned.1.call-update) | async-done | bytes 524304 | tf_op jit(solution)/shard_map/reduce_scatter | solution.py:31
  324.5 1.8 convert_bitcast_fusion
  326.3 0.0 all-gather.7.cloned.1.call-update
  326.3 0.0 all-gather.9.cloned.1.call-start
  326.4 0.5 all-gather.9.cloned.1.call-update
  326.9 0.0 copy-start
  326.9 0.0 all-gather.11.cloned.1.call-start
  327.0 26.9 %all-gather.7.cloned.1.call-done = bf16[256,4096]{0,1:T(8,128)(2,1)} async-done(((bf16[256,512]{0,1:T(8,128)(2,1)}), bf16[256,4096]{0,1:T(8,128)(2,1)}) %all-gather.7.cloned.1.call-update) | async-done | bytes 2097168 | tf_op jit(solution)/shard_map/all_gather | solution.py:37
  353.9 58.8 %all-gather.9.cloned.1.call-done = bf16[4096,512]{0,1:T(8,128)(2,1)} async-done(((bf16[256,512]{0,1:T(8,128)(2,1)}), bf16[4096,512]{0,1:T(8,128)(2,1)}) %all-gather.9.cloned.1.call-update) | async-done | bytes 4194320 | tf_op jit(solution)/shard_map/all_gather | solution.py:41
  412.6 4.8 %fusion.3 = bf16[256,512]{0,1:T(8,128)(2,1)} fusion(bf16[4096,512]{0,1:T(8,128)(2,1)} %all-gather.9.cloned.1.call-done, bf16[256,4096]{0,1:T(8,128)(2,1)} %all-gather.7.cloned.1.call-done, bf16[256,512]{0,1:T(8,128)(2,1)} %convert_bitcast_fusion), kind=kOutput, calls=%fused_computation.5 | convolution fusion | flops 1074397184 | bytes 6815744 | tf_op jit(solution)/shard_map/dot_general | solution.py:39
  417.4 0.0 all-gather.11.cloned.1.call-update
  417.5 25.8 %all-gather.11.cloned.1.call-done = bf16[256,4096]{0,1:T(8,128)(2,1)} async-done(((bf16[256,512]{0,1:T(8,128)(2,1)}), bf16[256,4096]{0,1:T(8,128)(2,1)}) %all-gather.11.cloned.1.call-update) | async-done | bytes 2097168 | tf_op jit(solution)/shard_map/all_gather | solution.py:49
  443.3 0.0 copy-done
  443.3 7.2 %fusion.1 = bf16[256,1024]{1,0:T(8,128)(2,1)} fusion(bf16[256,4096]{0,1:T(8,128)(2,1)} %all-gather.11.cloned.1.call-done, bf16[4096,1024]{1,0:T(8,128)(2,1)} %all-gather.5.cloned.1.call-done, bf16[256,1024]{1,0:T(8,128)(2,1)S(1)} %copy-done), kind=kOutput, calls=%fused_computation.2 | convolution fusion | flops 2148794368 | bytes 11534336 | tf_op jit(solution)/shard_map/dot_general | solution.py:48
Async XLA Ops:
  6.5 137.5 %reduce-scatter.3.cloned.1.call-start = ((), (), s32[]{:S(2)}) async-start(), calls=%async_computation.2 | async-start | bytes 17825792 | tf_op jit(solution)/shard_map/reduce_scatter | solution.py:20
  30.3 251.7 %all-gather.5.cloned.1.call-start = ((), (), s32[]{:S(2)}) async-start(), calls=%async_computation.3 | async-start | bytes 8912896 | tf_op jit(solution)/shard_map/all_gather | solution.py:29
  213.7 110.8 %reduce-scatter.5.cloned.1.call-start = ((), (), s32[]{:S(2)}) async-start(), calls=%async_computation.4 | async-start | bytes 4718592 | tf_op jit(solution)/shard_map/reduce_scatter | solution.py:31
  289.8 64.1 %all-gather.7.cloned.1.call-start = ((), (), s32[]{:S(2)}) async-start(), calls=%async_computation.5 | async-start | bytes 2359296 | tf_op jit(solution)/shard_map/all_gather | solution.py:37
  326.3 86.3 %all-gather.9.cloned.1.call-start = ((), (), s32[]{:S(2)}) async-start(), calls=%async_computation.6 | async-start | bytes 4456448 | tf_op jit(solution)/shard_map/all_gather | solution.py:41
  326.9 116.3 %copy-start = (bf16[256,1024]{1,0:T(8,128)(2,1)S(1)}, bf16[256,1024]{1,0:T(8,128)(2,1)}, u32[]{:S(2)}) copy-start(bf16[256,1024]{1,0:T(8,128)(2,1)} %multiply_convert_fusion) | copy-start | bytes 1572868
  326.9 116.3 %all-gather.11.cloned.1.call-start = ((), (), s32[]{:S(2)}) async-start(), calls=%async_computation.7 | async-start | bytes 2359296 | tf_op jit(solution)/shard_map/all_gather | solution.py:49
Sparse Core Ops, SparseCore 0:
  30.4 113.5 reduce-scatter.2
  213.9 68.1 all-gather.4
  289.9 34.5 reduce-scatter.4
  326.5 27.3 all-gather.6
  355.8 56.7 all-gather.8
  417.6 25.6 all-gather.10
where the time goes:
time: 458 us; the launch traced here: 457 us
  waiting for transfers between devices  329 us (72%)
  blocking collectives  64.8 us (14%)
  matrix products  43.5 us (9%)
  between operations  14.2 us (3%)
  other arithmetic  6 us (1%)
    reduce_scatter x1, waiting for transfers between devices, local(): lax.psum_scatter(lax.dot_general(section, activation, CONTRACT_FIRST, pre...  114 us
    all_gather x1, waiting for transfers between devices, local(): weight_column = lax.all_gather(normalized, 'dp', axis=0, tiled=True)  68.2 us
    psum x1, blocking collectives, local(): sum_squares = lax.psum(jnp.sum(gradient * gradient), ('dp', 'mp'))  64.8 us
    all_gather x1, waiting for transfers between devices, local(): lax.all_gather(gram_tile, 'dp', axis=0, tiled=True)  58.8 us
    reduce_scatter x1, waiting for transfers between devices, local(): lax.psum_scatter(lax.dot_general(section, normalized, CONTRACT_LAST, pref...  34.7 us
    all_gather x1, waiting for transfers between devices, local(): row_panel = lax.all_gather(gram_tile, 'mp', axis=1, tiled=True)  26.9 us
    all_gather x1, waiting for transfers between devices, local(): lax.all_gather(polynomial, 'mp', axis=1, tiled=True)  25.8 us
    dot_general x1, matrix products, local(): lax.dot_general(section, activation, CONTRACT_FIRST, preferred_element_ty...  23.7 us
  transfers between devices with their start and end apart: 6, of which 6 were waited for; matrix products, arithmetic and copies ran while one was open for 0% of the time, Pallas kernels for 0%

commit v1 on v0

--- a/solution.py
+++ b/solution.py
@@ -34,7 +34,12 @@
         scatter_dimension=0,
         tiled=True,
     ).T.astype(jnp.bfloat16)
-    row_panel = lax.all_gather(gram_tile, "mp", axis=1, tiled=True)
+    ring = [gram_tile]
+    for hop in range(7):
+        ring.append(lax.ppermute(ring[-1], "mp", [(dev, (dev + 1) % 8) for dev in range(8)]))
+    row_panel = jnp.roll(
+        jnp.concatenate(ring[::-1], axis=1), (lax.axis_index("mp") + 1) * ring[0].shape[1], axis=1
+    )
     section = row_panel
     square_tile = jnp.dot(
         section,

time: 458 us -> 434 us (0.948)
  waiting for transfers between devices: 329 us -> 289 us
  local copies, waits for them, and re-layouts: 0.01 us -> 10.2 us
    all_gather x1, waiting for transfers between devices: 58.8 us -> 0.41 us  [local(): lax.all_gather(gram_tile, 'dp', axis=0, tiled=True)]
    ppermute x0 -> x7, waiting for transfers between devices: none -> 42.4 us  [local(): lax.ppermute(ring[-1], 'mp', [(dev, (dev + 1) % 8) for dev in range(8)])]
    all_gather x1 -> x0, waiting for transfers between devices: 26.9 us -> none  [local(): row_panel = lax.all_gather(gram_tile, 'mp', axis=1, tiled=True)]
    unnamed x2 -> x20, local copies, waits for them, and re-layouts: 0.01 us -> 10.2 us
  transfers between devices with their start and end apart: 6 -> 12, of which waited for: 6 -> 12; matrix products, arithmetic and copies ran while one was open for 0% -> 3% of each run, Pallas kernels for 0% -> 0%
where the time goes in v1:
time: 434 us; the launch traced here: 433 us
  waiting for transfers between devices  289 us (67%)
  blocking collectives  64.8 us (15%)
  matrix products  43.5 us (10%)
  between operations  13.9 us (3%)
  local copies, waits for them, and re-layouts  10.2 us (2%)
  other arithmetic  7.5 us (2%)
  starting transfers between devices  4.71 us (1%)
    reduce_scatter x1, waiting for transfers between devices, local(): lax.psum_scatter(lax.dot_general(section, activation, CONTRACT_FIRST, pre...  114 us
    all_gather x1, waiting for transfers between devices, local(): weight_column = lax.all_gather(normalized, 'dp', axis=0, tiled=True)  68.2 us
    psum x1, blocking collectives, local(): sum_squares = lax.psum(jnp.sum(gradient * gradient), ('dp', 'mp'))  64.8 us
    ppermute x7, waiting for transfers between devices, local(): lax.ppermute(ring[-1], 'mp', [(dev, (dev + 1) % 8) for dev in range(8)])  42.4 us
    reduce_scatter x1, waiting for transfers between devices, local(): lax.psum_scatter(lax.dot_general(section, normalized, CONTRACT_LAST, pref...  34.5 us
    all_gather x1, waiting for transfers between devices, local(): lax.all_gather(polynomial, 'mp', axis=1, tiled=True)  29.6 us
    dot_general x1, matrix products, local(): lax.dot_general(section, activation, CONTRACT_FIRST, preferred_element_ty...  23.7 us
    unnamed x20, local copies, waits for them, and re-layouts  10.2 us
  transfers between devices with their start and end apart: 12, of which 12 were waited for; matrix products, arithmetic and copies ran while one was open for 3% of the time, Pallas kernels for 0%

profile of v1, /device:TPU:1, one launch (start us, length us, event | category | flops | bytes accessed | tf_op | source)
XLA Modules:
  0.0 433.4 jit_solution(1217112252482850628)
XLA Ops:
  6.5 0.0 reduce-scatter.3.cloned.1.call-start
  6.5 23.7 %fusion.14 = f32[4096,1024]{1,0:T(8,128)} fusion(bf16[2048,4096]{1,0:T(8,128)(2,1)} %param.2, bf16[2048,1024]{1,0:T(8,128)(2,1)} %param.3), kind=kOutput, calls=%fused_computation.28 | convolution fusion | flops 17179869184 | bytes 37748736 | tf_op jit(solution)/shard_map/dot_general | solution.py:21
  30.3 0.0 reduce-scatter.3.cloned.1.call-update
  30.3 0.0 all-gather.4.cloned.1.call-start
  30.3 113.7 %reduce-scatter.3.cloned.1.call-done = f32[256,1024]{1,0:T(8,128)} async-done(((f32[4096,1024]{1,0:T(8,128)}), f32[256,1024]{1,0:T(8,128)}) %reduce-scatter.3.cloned.1.call-update) | async-done | bytes 1048592 | tf_op jit(solution)/shard_map/reduce_scatter | solution.py:20
  144.0 2.1 multiply_reduce_fusion
  146.1 64.8 %psum.7 = f32[]{:T(128)} all-reduce(f32[]{:T(128)} %multiply_reduce_fusion), channel_id=1, replica_groups=mesh['dp'=16,'mp'=8] {'dp','mp'}, use_global_device_ids=true, to_apply=%region_2.0 | all-reduce | flops 1 | bytes 8 | tf_op jit(solution)/shard_map/psum | solution.py:26
  211.6 2.1 multiply_convert_fusion
  213.7 0.0 all-gather.4.cloned.1.call-update
  213.7 0.0 reduce-scatter.5.cloned.1.call-start
  213.8 68.2 %all-gather.4.cloned.1.call-done = bf16[4096,1024]{1,0:T(8,128)(2,1)} async-done(((bf16[256,1024]{1,0:T(8,128)(2,1)}), bf16[4096,1024]{1,0:T(8,128)(2,1)}) %all-gather.4.cloned.1.call-update) | async-done | bytes 8388624 | tf_op jit(solution)/shard_map/all_gather | solution.py:29
  282.0 7.8 %fusion.15 = f32[4096,256]{1,0:T(8,128)} fusion(bf16[4096,1024]{1,0:T(8,128)(2,1)} %all-gather.4.cloned.1.call-done, bf16[256,1024]{1,0:T(8,128)(2,1)} %multiply_convert_fusion), kind=kOutput, calls=%fused_computation.29 | convolution fusion | flops 2147483648 | bytes 13107200 | tf_op jit(solution)/shard_map/dot_general | solution.py:32
  289.8 0.0 reduce-scatter.5.cloned.1.call-update
  289.8 0.0 all-gather.6.cloned.1.call-start
  289.9 34.5 %reduce-scatter.5.cloned.1.call-done = f32[512,256]{1,0:T(8,128)} async-done(((f32[4096,256]{1,0:T(8,128)}), f32[512,256]{1,0:T(8,128)}) %reduce-scatter.5.cloned.1.call-update) | async-done | bytes 524304 | tf_op jit(solution)/shard_map/reduce_scatter | solution.py:31
  324.4 0.0 copy-start.1
  324.4 1.8 convert_bitcast_fusion
  326.2 0.0 all-gather.6.cloned.1.call-update
  326.3 0.0 all-gather.8.cloned.1.call-start
  326.3 1.2 collective-permute-start
  327.5 3.7 collective-permute-done
  331.2 2.3 collective-permute-start.1
  333.5 4.7 %collective-permute-done.1 = bf16[256,512]{0,1:T(8,128)(2,1)S(1)} collective-permute-done((bf16[256,512]{0,1:T(8,128)(2,1)S(1)}, bf16[256,512]{0,1:T(8,128)(2,1)S(1)}, u32[]{:S(2)}, u32[]{:S(2)}) %collective-permute-start.1) | collective-permute-done | bytes 262176 | tf_op jit(solution)/shard_map/ppermute | solution.py:39
  338.2 1.1 collective-permute-start.2
  339.3 5.9 %collective-permute-done.2 = bf16[256,512]{0,1:T(8,128)(2,1)S(1)} collective-permute-done((bf16[256,512]{0,1:T(8,128)(2,1)S(1)}, bf16[256,512]{0,1:T(8,128)(2,1)S(1)}, u32[]{:S(2)}, u32[]{:S(2)}) %collective-permute-start.2) | collective-permute-done | bytes 262176 | tf_op jit(solution)/shard_map/ppermute | solution.py:39
  345.2 0.0 collective-permute-start.3
  345.2 7.0 %collective-permute-done.3 = bf16[256,512]{0,1:T(8,128)(2,1)S(1)} collective-permute-done((bf16[256,512]{0,1:T(8,128)(2,1)S(1)}, bf16[256,512]{0,1:T(8,128)(2,1)S(1)}, u32[]{:S(2)}, u32[]{:S(2)}) %collective-permute-start.3) | collective-permute-done | bytes 262176 | tf_op jit(solution)/shard_map/ppermute | solution.py:39
  352.2 0.0 collective-permute-start.4
  352.2 7.0 %collective-permute-done.4 = bf16[256,512]{0,1:T(8,128)(2,1)S(1)} collective-permute-done((bf16[256,512]{0,1:T(8,128)(2,1)S(1)}, bf16[256,512]{0,1:T(8,128)(2,1)S(1)}, u32[]{:S(2)}, u32[]{:S(2)}) %collective-permute-start.4) | collective-permute-done | bytes 262176 | tf_op jit(solution)/shard_map/ppermute | solution.py:39
  359.3 0.0 collective-permute-start.5
  359.3 7.0 %collective-permute-done.5 = bf16[256,512]{0,1:T(8,128)(2,1)S(1)} collective-permute-done((bf16[256,512]{0,1:T(8,128)(2,1)S(1)}, bf16[256,512]{0,1:T(8,128)(2,1)S(1)}, u32[]{:S(2)}, u32[]{:S(2)}) %collective-permute-start.5) | collective-permute-done | bytes 262176 | tf_op jit(solution)/shard_map/ppermute | solution.py:39
  366.3 0.0 collective-permute-start.6
  366.3 7.0 %collective-permute-done.6 = bf16[256,512]{0,1:T(8,128)(2,1)S(1)} collective-permute-done((bf16[256,512]{0,1:T(8,128)(2,1)S(1)}, bf16[256,512]{0,1:T(8,128)(2,1)S(1)}, u32[]{:S(2)}, u32[]{:S(2)}) %collective-permute-start.6) | collective-permute-done | bytes 262176 | tf_op jit(solution)/shard_map/ppermute | solution.py:39
  373.3 0.7 constant_dynamic-update-slice_fusion.15
  374.0 0.0 copy-start.2
  374.0 0.7 constant_dynamic-update-slice_fusion.14
  374.7 0.7 constant_dynamic-update-slice_fusion.13
  375.5 0.7 constant_dynamic-update-slice_fusion.12
  376.2 0.7 constant_dynamic-update-slice_fusion.11
  376.9 0.7 constant_dynamic-update-slice_fusion.10
  377.6 0.7 constant_dynamic-update-slice_fusion.9
  378.3 0.0 copy-done.1
  378.3 0.7 constant_dynamic-update-slice_fusion.8
  379.1 0.7 constant_dynamic-update-slice_fusion.7
  379.8 0.7 constant_dynamic-update-slice_fusion.6
  380.5 0.7 constant_dynamic-update-slice_fusion.5
  381.3 0.7 constant_dynamic-update-slice_fusion.4
  382.0 0.7 constant_dynamic-update-slice_fusion.3
  382.7 0.7 constant_dynamic-update-slice_fusion.2
  383.4 0.7 constant_dynamic-update-slice_fusion.1
  384.2 0.7 constant_dynamic-update-slice_fusion
  384.9 0.0 copy-start
  384.9 0.4 all-gather.6.cloned.1.call-done
  385.3 0.0 copy-done.2
  385.3 4.8 %fusion.10 = bf16[256,512]{0,1:T(8,128)(2,1)} fusion(bf16[4096,512]{0,1:T(8,128)(2,1)} %all-gather.6.cloned.1.call-done, bf16[256,8192]{0,1:T(8,128)(2,1)} %constant_dynamic-update-slice_fusion, s32[]{:T(128)S(6)} %select_n.14, bf16[256,512]{0,1:T(8,128)(2,1)S(1)} %copy-done.2), kind=kOutput, calls=%fused_computation.7 | convolution fusion | flops 1074397184 | bytes 6815748 | tf_op jit(solution)/shard_map/dot_general | solution.py:44
  390.1 0.0 all-gather.8.cloned.1.call-update
  390.1 29.6 %all-gather.8.cloned.1.call-done = bf16[256,4096]{0,1:T(8,128)(2,1)} async-done(((bf16[256,512]{0,1:T(8,128)(2,1)}), bf16[256,4096]{0,1:T(8,128)(2,1)}) %all-gather.8.cloned.1.call-update) | async-done | bytes 2097168 | tf_op jit(solution)/shard_map/all_gather | solution.py:54
  419.7 0.0 copy-done
  419.7 7.2 %fusion.3 = bf16[256,1024]{1,0:T(8,128)(2,1)} fusion(bf16[256,4096]{0,1:T(8,128)(2,1)} %all-gather.8.cloned.1.call-done, bf16[4096,1024]{1,0:T(8,128)(2,1)} %all-gather.4.cloned.1.call-done, bf16[256,1024]{1,0:T(8,128)(2,1)S(1)} %copy-done), kind=kOutput, calls=%fused_computation.4 | convolution fusion | flops 2148794368 | bytes 11534336 | tf_op jit(solution)/shard_map/dot_general | solution.py:53
Async XLA Ops:
  6.5 137.5 %reduce-scatter.3.cloned.1.call-start = ((), (), s32[]{:S(2)}) async-start(), calls=%async_computation.2 | async-start | bytes 17825792 | tf_op jit(solution)/shard_map/reduce_scatter | solution.py:20
  30.3 251.7 %all-gather.4.cloned.1.call-start = ((), (), s32[]{:S(2)}) async-start(), calls=%async_computation.3 | async-start | bytes 8912896 | tf_op jit(solution)/shard_map/all_gather | solution.py:29
  213.7 110.7 %reduce-scatter.5.cloned.1.call-start = ((), (), s32[]{:S(2)}) async-start(), calls=%async_computation.4 | async-start | bytes 4718592 | tf_op jit(solution)/shard_map/reduce_scatter | solution.py:31
  289.8 95.5 %all-gather.6.cloned.1.call-start = ((), (), s32[]{:S(2)}) async-start(), calls=%async_computation.5 | async-start | bytes 4456448 | tf_op jit(solution)/shard_map/all_gather | solution.py:46
  324.4 53.9 %copy-start.1 = (f32[512,256]{1,0:T(8,128)S(1)}, f32[512,256]{1,0:T(8,128)}, u32[]{:S(2)}) copy-start(f32[512,256]{1,0:T(8,128)} %reduce-scatter.5.cloned.1.call-done) | copy-start | bytes 1572868
  326.3 93.4 %all-gather.8.cloned.1.call-start = ((), (), s32[]{:S(2)}) async-start(), calls=%async_computation.6 | async-start | bytes 2359296 | tf_op jit(solution)/shard_map/all_gather | solution.py:54
  326.3 4.9 %collective-permute-start = (bf16[256,512]{0,1:T(8,128)(2,1)}, bf16[256,512]{0,1:T(8,128)(2,1)S(1)}, u32[]{:S(2)}, u32[]{:S(2)}) collective-permute-start(bf16[256,512]{0,1:T(8,128)(2,1)} %convert_bitcast_fusion), channel_id=1, source_target_pairs={{0,1},{1,2},{2,3},{3,4},{4,5},{5,6},{6,7},{7,0},{8,9},{9,10},{10,1... | collective-permute-start | bytes 786440 | tf_op jit(solution)/shard_map/ppermute | solution.py:39
  331.2 7.0 %collective-permute-start.1 = (bf16[256,512]{0,1:T(8,128)(2,1)S(1)}, bf16[256,512]{0,1:T(8,128)(2,1)S(1)}, u32[]{:S(2)}, u32[]{:S(2)}) collective-permute-start(bf16[256,512]{0,1:T(8,128)(2,1)S(1)} %collective-permute-done), channel_id=1, source_target_pairs={{0,1},{1,2},{2,3},{3,4},{4,5},{5,6},{6,7},{7,0},{8,9},{9,10},{10,1... | collective-permute-start | bytes 786440 | tf_op jit(solution)/shard_map/ppermute | solution.py:39
  338.2 7.0 %collective-permute-start.2 = (bf16[256,512]{0,1:T(8,128)(2,1)S(1)}, bf16[256,512]{0,1:T(8,128)(2,1)S(1)}, u32[]{:S(2)}, u32[]{:S(2)}) collective-permute-start(bf16[256,512]{0,1:T(8,128)(2,1)S(1)} %collective-permute-done.1), channel_id=1, source_target_pairs={{0,1},{1,2},{2,3},{3,4},{4,5},{5,6},{6,7},{7,0},{8,9},{9,10},{10,1... | collective-permute-start | bytes 786440 | tf_op jit(solution)/shard_map/ppermute | solution.py:39
  345.2 7.0 %collective-permute-start.3 = (bf16[256,512]{0,1:T(8,128)(2,1)S(1)}, bf16[256,512]{0,1:T(8,128)(2,1)S(1)}, u32[]{:S(2)}, u32[]{:S(2)}) collective-permute-start(bf16[256,512]{0,1:T(8,128)(2,1)S(1)} %collective-permute-done.2), channel_id=1, source_target_pairs={{0,1},{1,2},{2,3},{3,4},{4,5},{5,6},{6,7},{7,0},{8,9},{9,10},{10,1... | collective-permute-start | bytes 786440 | tf_op jit(solution)/shard_map/ppermute | solution.py:39
  352.2 7.0 %collective-permute-start.4 = (bf16[256,512]{0,1:T(8,128)(2,1)S(1)}, bf16[256,512]{0,1:T(8,128)(2,1)S(1)}, u32[]{:S(2)}, u32[]{:S(2)}) collective-permute-start(bf16[256,512]{0,1:T(8,128)(2,1)S(1)} %collective-permute-done.3), channel_id=1, source_target_pairs={{0,1},{1,2},{2,3},{3,4},{4,5},{5,6},{6,7},{7,0},{8,9},{9,10},{10,1... | collective-permute-start | bytes 786440 | tf_op jit(solution)/shard_map/ppermute | solution.py:39
  359.3 7.0 %collective-permute-start.5 = (bf16[256,512]{0,1:T(8,128)(2,1)S(1)}, bf16[256,512]{0,1:T(8,128)(2,1)S(1)}, u32[]{:S(2)}, u32[]{:S(2)}) collective-permute-start(bf16[256,512]{0,1:T(8,128)(2,1)S(1)} %collective-permute-done.4), channel_id=1, source_target_pairs={{0,1},{1,2},{2,3},{3,4},{4,5},{5,6},{6,7},{7,0},{8,9},{9,10},{10,1... | collective-permute-start | bytes 786440 | tf_op jit(solution)/shard_map/ppermute | solution.py:39
  366.3 7.0 %collective-permute-start.6 = (bf16[256,512]{0,1:T(8,128)(2,1)S(1)}, bf16[256,512]{0,1:T(8,128)(2,1)S(1)}, u32[]{:S(2)}, u32[]{:S(2)}) collective-permute-start(bf16[256,512]{0,1:T(8,128)(2,1)S(1)} %collective-permute-done.5), channel_id=1, source_target_pairs={{0,1},{1,2},{2,3},{3,4},{4,5},{5,6},{6,7},{7,0},{8,9},{9,10},{10,1... | collective-permute-start | bytes 786440 | tf_op jit(solution)/shard_map/ppermute | solution.py:39
  374.0 11.3 %copy-start.2 = (bf16[256,512]{0,1:T(8,128)(2,1)S(1)}, bf16[256,512]{0,1:T(8,128)(2,1)}, u32[]{:S(2)}) copy-start(bf16[256,512]{0,1:T(8,128)(2,1)} %convert_bitcast_fusion) | copy-start | bytes 786436
  384.9 34.8 %copy-start = (bf16[256,1024]{1,0:T(8,128)(2,1)S(1)}, bf16[256,1024]{1,0:T(8,128)(2,1)}, u32[]{:S(2)}) copy-start(bf16[256,1024]{1,0:T(8,128)(2,1)} %multiply_convert_fusion) | copy-start | bytes 1572868
Sparse Core Ops, SparseCore 0:
  30.4 113.5 reduce-scatter.2
  213.8 68.1 all-gather.3
  289.9 34.4 reduce-scatter.4
  326.4 58.8 all-gather.5
  390.2 29.3 all-gather.7
